TPU v7x, 32 devices: a whole 2x2x4 slice. The times are simulated.
32 devices in a mesh: patch: 16 (over z, y, core), chan: 2 (over x).
Axes of the slice: x: 2, y: 2, z: 4, core: 2. Of those that a mesh axis runs over, the one named last changes fastest.
Arguments:
- fields: bfloat16 [16, 128, 1024], P('patch', 'chan'), may hold values from -6 to 6
- w_one: bfloat16 [9, 512, 128], P(None, 'chan'), may hold values from -0.1875 to 0.1875
- bias_one: float32 [512], P('chan'), may hold values from -3 to 3
- w_two: bfloat16 [9, 128, 512], P(None, None, 'chan'), may hold values from -0.09375 to 0.09375
- neighbour: int32 [16, 4], replicated, may hold values from 0 to 15, as said below
- seam_code: int32 [16, 4], replicated, may hold values from 0 to 7, as said below
- band_order: int32 [16], replicated, may hold values from 0 to 15, each once
- target: bfloat16 [16, 128, 1024], P('patch', 'chan'), may hold values from -6 to 6
- lat_weight: bfloat16 [16, 1024], P('patch'), may hold values from 0.099609375 to 1
Outputs:
- loss_value: float32 [], replicated
- grad_one: float32 [9, 512, 128], P(None, 'chan')
- grad_two: float32 [9, 128, 512], P(None, None, 'chan')
- grad_bias: float32 [512], P('chan')
Inputs may be any that keep to these rules, and one draw needn't show every extreme that they name: The sides of all patches are paired: side s of patch p borders side t = seam_code[p, s] mod 4 of patch q = neighbour[p, s], and then neighbour[q, t] = p, seam_code[q, t] mod 4 = s, and both codes agree on being 4 or more; so every edge is read by exactly one side of one other patch, and the four sides of a patch face four different patches. `seam_code`: code mod 4 names the neighbour's edge that forms the seam; codes 4 and above run that edge reversed, alike on both sides of a seam. `band_order`: each patch fills exactly one slot of every band.
All inputs are finite; a program needn't handle non-finite values.
Results may differ from a plain program's by a relative error of at most 0.0021.
Values may be sent and summed in bfloat16 or wider, within the bound.
A program may use at most 64 MiB of HBM per device.

v0:
```python
import math
import jax
import jax.numpy as jnp
from jax import lax
from jax.sharding import PartitionSpec as P

C = 128
P_SIZE = 32


def edges_of(field):
    return jnp.stack(
        [field[..., 0, :], field[..., -1, :], field[..., :, 0], field[..., :, -1]], axis=-3
    )


def with_frame(field, strips):
    padded = jnp.pad(field, ((0, 0), (1, 1), (1, 1)))
    padded = padded.at[:, 0, 1:-1].set(strips[0])
    padded = padded.at[:, -1, 1:-1].set(strips[1])
    padded = padded.at[:, 1:-1, 0].set(strips[2])
    padded = padded.at[:, 1:-1, -1].set(strips[3])
    return padded


def tap_list(padded):
    length = padded.shape[-1] - 2
    span = length + 2
    flat = jnp.pad(padded.reshape(padded.shape[0], span * span), ((0, 0), (0, 2)))
    return [
        flat[:, row_off * span + col_off : row_off * span + col_off + length * span]
        for row_off in range(3)
        for col_off in range(3)
    ]


def narrow(wide, length):
    return wide.reshape(wide.shape[0], length, length + 2)[:, :, :length].reshape(
        wide.shape[0], length * length
    )


def widen(values, length):
    shaped = values.reshape(values.shape[0], length, length)
    return jnp.pad(shaped, ((0, 0), (0, 0), (0, 2))).reshape(values.shape[0], length * (length + 2))


def apply_taps(weight, taps):
    summed = jnp.zeros((weight.shape[1], taps[0].shape[1]), jnp.float32)
    for tap_index in range(9):
        summed = summed + jnp.dot(
            weight[tap_index], taps[tap_index], preferred_element_type=jnp.float32
        )
    return summed


def smooth_gate(values):
    return jax.nn.gelu(values, approximate=True)


def oriented(strips, codes):
    return jnp.where((codes >= 4)[:, None, None], strips[..., ::-1], strips)


def on_device(fields, w_one, bias_one, w_two, neighbour, seam_code, band_order, target, lat_weight):
    length = P_SIZE
    span = P_SIZE + 2
    cell_count = P_SIZE * P_SIZE
    patch_count = lax.axis_size("patch")
    part_len = cell_count // patch_count
    own_index = lax.axis_index("patch")
    own_nbr = lax.dynamic_slice_in_dim(neighbour, own_index, 1, 0)[0]
    own_code = lax.dynamic_slice_in_dim(seam_code, own_index, 1, 0)[0]
    sides = jnp.arange(4, dtype=jnp.int32)

    def pick_edges(shard_rows):
        row_ids = jnp.arange(shard_rows.shape[0], dtype=jnp.int32)
        chosen = (own_nbr[:, None, None] == row_ids[None, :, None]) & (
            (own_code % 4)[:, None, None] == sides[None, None, :]
        )
        return jnp.einsum(
            "srt,rtcq->scq",
            chosen.astype(shard_rows.dtype),
            shard_rows,
            preferred_element_type=jnp.float32,
        )

    local = fields[0]
    local_ch = local.shape[0]
    whole = lax.all_gather(local, "chan", axis=0, tiled=True)
    grid = whole.reshape(whole.shape[0], length, length)
    seams = pick_edges(lax.all_gather(edges_of(grid)[None], "patch", axis=0, tiled=True))
    x_pad = with_frame(grid, oriented(seams, own_code).astype(jnp.bfloat16))
    x_taps = tap_list(x_pad)
    preact = narrow(apply_taps(w_one, x_taps), length) + bias_one[:, None]
    hidden = smooth_gate(preact).astype(jnp.bfloat16)
    inner_ch = hidden.shape[0]
    hidden_grid = hidden.reshape(inner_ch, length, length)
    hidden_seams = pick_edges(
        lax.all_gather(edges_of(hidden_grid)[None], "patch", axis=0, tiled=True)
    )
    hidden_strips = oriented(hidden_seams, own_code).astype(jnp.bfloat16)
    h_pad = with_frame(hidden_grid, hidden_strips)
    h_taps = tap_list(h_pad)
    mixed = lax.psum_scatter(
        narrow(apply_taps(w_two, h_taps), length), "chan", scatter_dimension=0, tiled=True
    )
    outputs = local.astype(jnp.float32) + mixed
    inv_root = 1.0 / math.sqrt(patch_count * cell_count)
    inverse = (
        jnp.zeros((patch_count,), jnp.int32)
        .at[band_order]
        .set(jnp.arange(patch_count, dtype=jnp.int32))
    )
    arrived = lax.all_to_all(
        outputs.reshape(local_ch, patch_count, part_len),
        "patch",
        split_axis=1,
        concat_axis=1,
        tiled=True,
    )
    in_band = arrived[:, band_order, :].reshape(local_ch, cell_count)
    misfit = in_band - target[0].astype(jnp.float32)
    lat_w = lat_weight[0].astype(jnp.float32)[None, :]
    partial_loss = jnp.sum(lat_w * misfit * misfit)
    band_grad = (
        (lat_w * misfit * inv_root).astype(jnp.bfloat16).reshape(local_ch, patch_count, part_len)
    )
    returned = lax.all_to_all(
        band_grad[:, inverse, :], "patch", split_axis=1, concat_axis=1, tiled=True
    )
    grad_out = returned.reshape(local_ch, cell_count)
    loss_value = lax.psum(partial_loss, ("patch", "chan")) / (patch_count * cell_count * C)
    grad_full = lax.all_gather(grad_out, "chan", axis=0, tiled=True)
    grad_wide = widen(grad_full, length)
    flat_len = span * span + 2
    wide_len = length * span
    frame_flat = jnp.zeros((inner_ch, flat_len), jnp.float32)
    tap_index = 0
    for row_off in range(3):
        for col_off in range(3):
            block = lax.dot_general(
                w_two[tap_index],
                grad_wide,
                (((0,), (0,)), ((), ())),
                preferred_element_type=jnp.float32,
            )
            offset = row_off * span + col_off
            frame_flat = frame_flat + jnp.pad(
                block, ((0, 0), (offset, flat_len - offset - wide_len))
            )
            tap_index = tap_index + 1
    grad_frame = frame_flat[:, : span * span].reshape(inner_ch, span, span)
    interior = grad_frame[:, 1:-1, 1:-1]
    frames = jnp.stack(
        [
            grad_frame[:, 0, 1:-1],
            grad_frame[:, -1, 1:-1],
            grad_frame[:, 1:-1, 0],
            grad_frame[:, 1:-1, -1],
        ]
    )
    shard_rows = lax.all_gather(frames[None], "patch", axis=0, tiled=True)
    matched = (neighbour == own_index)[:, :, None] & (
        (seam_code % 4)[:, :, None] == sides[None, None, :]
    )
    keep_same = (matched & (seam_code < 4)[:, :, None]).astype(jnp.float32)
    keep_turned = (matched & (seam_code >= 4)[:, :, None]).astype(jnp.float32)
    running = jnp.einsum("rst,rsep->tep", keep_same, shard_rows, precision=lax.Precision.HIGHEST)
    edge_back = running + jnp.einsum(
        "rst,rsep->tep", keep_turned, shard_rows[..., ::-1], precision=lax.Precision.HIGHEST
    )
    grad_h = interior.at[:, 0, :].add(edge_back[0])
    grad_h = grad_h.at[:, -1, :].add(edge_back[1])
    grad_h = grad_h.at[:, :, 0].add(edge_back[2])
    grad_h = grad_h.at[:, :, -1].add(edge_back[3])
    grad_h = grad_h.reshape(inner_ch, cell_count)
    grad_pre = jax.vjp(smooth_gate, preact)[1](grad_h)[0]
    bias_local = jnp.sum(grad_pre, axis=1)
    pre_wide = widen(grad_pre.astype(jnp.bfloat16), length)
    one_local = jnp.stack(
        [
            lax.dot_general(
                pre_wide, x_taps[idx], (((1,), (1,)), ((), ())), preferred_element_type=jnp.float32
            )
            for idx in range(9)
        ]
    )
    two_local = jnp.stack(
        [
            lax.dot_general(
                grad_wide, h_taps[idx], (((1,), (1,)), ((), ())), preferred_element_type=jnp.float32
            )
            for idx in range(9)
        ]
    )
    grad_one, grad_two, grad_bias = lax.psum((one_local, two_local, bias_local), "patch")
    return (loss_value, grad_one, grad_two, grad_bias)


def solution(mesh):
    placed = (
        P("patch", "chan", None),
        P(None, "chan", None),
        P("chan"),
        P(None, None, "chan"),
        P(),
        P(),
        P(),
        P("patch", "chan", None),
        P("patch", None),
    )
    return jax.shard_map(
        on_device,
        mesh=mesh,
        in_specs=placed,
        out_specs=(P(), P(None, "chan", None), P(None, None, "chan"), P("chan")),
        check_vma=False,
    )
```

profile of v0, /device:TPU:0, one launch (start us, length us, event | category | flops | bytes accessed | tf_op | source)
XLA Modules:
  0.0 331.3 jit_solution(5937897365871116879)
XLA Ops:
  7.2 7.4 %all-gather = bf16[1,128,1024]{2,1,0:T(8,128)(2,1)S(1)} all-gather(bf16[1,64,1024]{2,1,0:T(8,128)(2,1)} %param.33), channel_id=2, replica_groups=mesh['patch'=16,'chan'=2] {'chan'}, dimensions={1}, use_global_device_ids=true | all-gather | bytes 393216 | tf_op jit(solution)/shard_map/all_gather | solution.py:90
  15.8 23.5 %all-gather.1 = bf16[64,128,32]{1,2,0:T(8,128)(2,1)S(1)} all-gather(bf16[4,128,32]{1,2,0:T(8,128)(2,1)S(1)} %pad_maximum_fusion.2), channel_id=3, replica_groups=mesh['patch'=16,'chan'=2] {'patch'}, dimensions={0}, use_global_device_ids=true | all-gather | bytes 557056 | tf_op jit(solution)/shard_map/all_gather | solution.py:92
  40.6 1.5 scatter.34
  47.8 35.0 %all-gather.7.cloned.1.call-done = bf16[64,256,32]{1,2,0:T(8,128)(2,1)} async-done(((bf16[4,256,32]{1,2,0:T(8,128)(2,1)}), bf16[64,256,32]{1,2,0:T(8,128)(2,1)}) %all-gather.7.cloned.1.call-update) | async-done | bytes 1048592 | tf_op jit(solution)/shard_map/all_gather | solution.py:100
  82.7 2.0 convolution_bitcast_fusion.27
  85.0 1.5 scatter.40
  91.5 13.4 %reduce-scatter.4.cloned.1.call-done = f32[64,1024]{1,0:T(8,128)} async-done(((f32[128,1024]{1,0:T(8,128)}), f32[64,1024]{1,0:T(8,128)}) %reduce-scatter.4.cloned.1.call-update) | async-done | bytes 262160
  104.9 1.1 copy.94
  107.4 5.6 %all-to-all-start = ((f32[16,1,4096]{2,1,0:T(1,128)}), f32[16,1,4096]{2,1,0:T(1,128)S(1)}, u32[]{:S(2)}, u32[]{:S(2)}) async-start(f32[16,1,4096]{2,1,0:T(1,128)} %reshape.635), calls=%async_computation | async-start | bytes 524288 | tf_op jit(solution)/shard_map/all_to_all | solution.py:115
  114.0 9.1 %all-to-all-done = f32[16,1,4096]{2,1,0:T(1,128)S(1)} async-done(((f32[16,1,4096]{2,1,0:T(1,128)}), f32[16,1,4096]{2,1,0:T(1,128)S(1)}, u32[]{:S(2)}, u32[]{:S(2)}) %all-to-all-start) | async-done | bytes 262176 | tf_op jit(solution)/shard_map/all_to_all | solution.py:115
  123.6 1.3 reduce.35
  125.9 1.6 gather_fusion
  128.6 10.7 %all_to_all.10 = bf16[16,2,2048]{2,1,0:T(2,128)(2,1)S(1)} all-to-all(bf16[16,2,2048]{2,1,0:T(2,128)(2,1)S(1)} %reshape.637), channel_id=1, replica_groups=mesh['patch'=16,'chan'=2] {'patch'}, dimensions={0} | all-to-all | bytes 262144 | tf_op jit(solution)/shard_map/all_to_all | solution.py:129
  139.9 5.6 %all_gather.18 = bf16[128,1024]{1,0:T(8,128)(2,1)S(1)} all-gather(bf16[64,1024]{1,0:T(8,128)(2,1)S(1)} %reshape.572), channel_id=1, replica_groups=mesh['patch'=16,'chan'=2] {'chan'}, dimensions={0}, use_global_device_ids=true | all-gather | bytes 393216 | tf_op jit(solution)/shard_map/all_gather | solution.py:134
  147.5 1.2 convolution_bitcast_fusion.6
  151.2 1.7 pad_add_fusion
  152.9 2.5 reshape.575
  156.2 1.1 slice_bitcast_fusion.3
  158.3 2.4 slice.614
  169.4 27.6 %all-gather.9.cloned.1.call-done = f32[64,256,32]{1,2,0:T(8,128)} async-done(((f32[4,256,32]{1,2,0:T(8,128)}), f32[64,256,32]{1,2,0:T(8,128)}) %all-gather.9.cloned.1.call-update) | async-done | bytes 2097168 | tf_op jit(solution)/shard_map/all_gather | solution.py:163
  197.0 3.9 %rev.11 = f32[16,4,256,32]{2,3,1,0:T(8,128)} reverse(f32[16,4,256,32]{2,3,1,0:T(8,128)} %bitcast.319), dimensions={3} | reverse | bytes 4194304 | tf_op jit(solution)/shard_map/rev | solution.py:171
  200.8 3.6 %fusion.6 = f32[4,256,32]{1,0,2:T(4,128)S(1)} fusion(f32[16,4,256,32]{2,3,1,0:T(8,128)} %bitcast.320, s32[16,4]{0,1:T(4,128)S(1)} %add_select_fusion, pred[16,4]{0,1:T(4,128)(4,1)S(1)} %get-tuple-element.175, pred[16,4]{0,1:T(4,128)(4,1)S(1)} %get-tuple-element.182), kind=kOutput, calls=%fused_computation.43 | convolution fusion | flops 25166592 | bytes 2228608 | tf_op jit(solution)/shard_map/rst,rsep->tep/dot_general | solution.py:169
  204.5 2.0 fusion.30
  206.6 1.4 fusion.134
  208.0 1.4 fusion.133
  210.3 1.8 scatter-add.16
  213.1 1.8 scatter-add.19
  214.9 2.0 fusion.168
  223.2 38.6 %psum.28 = f32[]{:T(128)} all-reduce(f32[]{:T(128)} %fusion.59), channel_id=1, replica_groups=mesh['patch'=16,'chan'=2] {'patch','chan'}, use_global_device_ids=true, to_apply=%region_2.3 | all-reduce | flops 1 | bytes 8 | tf_op jit(solution)/shard_map/psum | solution.py:133
  262.4 32.4 %psum.31 = f32[256]{0:T(256)} all-reduce(f32[256]{0:T(256)S(1)} %get-tuple-element.150), channel_id=1, replica_groups=mesh['patch'=16,'chan'=2] {'patch'}, use_global_device_ids=true, to_apply=%region_7.8 | all-reduce | flops 256 | bytes 2048 | tf_op jit(solution)/shard_map/psum | solution.py:197
  294.8 25.3 %all-reduce.18.cloned.1.call-done = (f32[9,256,128]{2,1,0:T(8,128)}, f32[9,128,256]{2,1,0:T(8,128)}) async-done(((f32[9,256,128]{2,1,0:T(8,128)}, f32[9,128,256]{2,1,0:T(8,128)}), (f32[9,256,128]{2,1,0:T(8,128)}, f32[9,128,256]{2,1,0:T(8,128)})) %all-reduce.18.cloned.1.call-update) | async-done | bytes 2359312 | tf_op jit(solution)/shard_map/psum | solution.py:197
  320.2 2.5 copy.182
  (164 shorter events, 42.6 us)
Async XLA Ops:
  7.2 75.6 %all-gather.7.cloned.1.call-start = ((), (), s32[]{:S(2)}) async-start(), calls=%async_computation.3 | async-start | bytes 1114112 | tf_op jit(solution)/shard_map/all_gather | solution.py:100
  39.2 3.4 %copy-start.5 = (bf16[9,256,128]{2,1,0:T(8,128)(2,1)S(1)}, bf16[9,256,128]{2,1,0:T(8,128)(2,1)}, u32[]{:S(2)}) copy-start(bf16[9,256,128]{2,1,0:T(8,128)(2,1)} %param.34) | copy-start | bytes 1769476
  45.5 0.7 copy-start.12
  47.4 57.6 %reduce-scatter.4.cloned.1.call-start = ((), (), s32[]{:S(2)}) async-start(), calls=%async_computation.5 | async-start | bytes 786432
  84.7 2.5 copy-start.1
  90.2 1.0 copy-start.6
  90.3 1.2 copy-start.13
  106.1 6.9 %copy-start.10 = (bf16[1,1024]{1,0:T(2,128)(2,1)S(1)}, bf16[1,1024]{1,0:T(2,128)(2,1)}, u32[]{:S(2)}) copy-start(bf16[1,1024]{1,0:T(2,128)(2,1)} %param.41) | copy-start | bytes 6148
  106.1 7.0 %copy-start.7 = (bf16[1,64,1024]{2,1,0:T(8,128)(2,1)S(1)}, bf16[1,64,1024]{2,1,0:T(8,128)(2,1)}, u32[]{:S(2)}) copy-start(bf16[1,64,1024]{2,1,0:T(8,128)(2,1)} %param.40) | copy-start | bytes 393220
  107.4 15.7 %all-to-all-start = ((f32[16,1,4096]{2,1,0:T(1,128)}), f32[16,1,4096]{2,1,0:T(1,128)S(1)}, u32[]{:S(2)}, u32[]{:S(2)}) async-start(f32[16,1,4096]{2,1,0:T(1,128)} %reshape.635), calls=%async_computation | async-start | bytes 524288 | tf_op jit(solution)/shard_map/all_to_all | solution.py:115
  113.0 84.0 %all-gather.9.cloned.1.call-start = ((), (), s32[]{:S(2)}) async-start(), calls=%async_computation.4 | async-start | bytes 2228224 | tf_op jit(solution)/shard_map/all_gather | solution.py:163
  147.4 1.2 copy-start.2
  152.9 5.3 %copy-start.9 = (s32[16,4]{0,1:T(4,128)S(1)}, s32[16,4]{0,1:T(4,128)}, u32[]{:S(2)}) copy-start(s32[16,4]{0,1:T(4,128)} %param.38) | copy-start | bytes 772
  152.9 5.4 %copy-start.11 = (s32[16,4]{0,1:T(4,128)S(1)}, s32[16,4]{0,1:T(4,128)}, u32[]{:S(2)}) copy-start(s32[16,4]{0,1:T(4,128)} %param.37) | copy-start | bytes 772
  158.2 162.0 %all-reduce.18.cloned.1.call-start = ((), (), s32[]{:S(2)}) async-start(), calls=%async_computation.6 | async-start | bytes 4718592 | tf_op jit(solution)/shard_map/psum | solution.py:197
  200.8 3.6 %copy-start = (f32[16,4,256,32]{2,3,1,0:T(8,128)S(1)}, f32[16,4,256,32]{2,3,1,0:T(8,128)}, u32[]{:S(2)}) copy-start(f32[16,4,256,32]{2,3,1,0:T(8,128)} %rev.11) | copy-start | bytes 6291460
  220.6 1.0 copy-start.4
  221.6 0.9 copy-start.8
  320.2 2.5 copy-start.3
Sparse Core Ops, SparseCore 0:
  47.5 35.2 all-gather.6
  91.4 13.4 reduce-scatter.3
  158.3 38.5 all-gather.8
  221.7 98.3 all-reduce.17
where the time goes:
time: 332 us; the launch traced here: 331 us
  blocking collectives  118 us (36%)
  waiting for transfers between devices  110 us (33%)
  local copies, waits for them, and re-layouts  38.7 us (12%)
  matrix products  29.4 us (9%)
  between operations  16.4 us (5%)
  other arithmetic  12.4 us (4%)
  starting transfers between devices  5.79 us (2%)
    psum x1, blocking collectives, on_device(): lax.psum(partial_loss, ('patch', 'chan')) / (patch_count * cell_count * C)  38.6 us
    all_gather x1, waiting for transfers between devices, on_device(): lax.all_gather(edges_of(hidden_grid)[None], 'patch', axis=0, tiled=True)  35 us
    psum x1, blocking collectives, on_device(): lax.psum((one_local, two_local, bias_local), 'patch')  32.4 us
    all_gather x1, waiting for transfers between devices, on_device(): shard_rows = lax.all_gather(frames[None], 'patch', axis=0, tiled=True)  27.6 us
    psum x1, waiting for transfers between devices, on_device(): lax.psum((one_local, two_local, bias_local), 'patch')  25.3 us
    all_gather x1, blocking collectives, on_device(): lax.all_gather(edges_of(grid)[None], 'patch', axis=0, tiled=True)  23.5 us
    unnamed x5, waiting for transfers between devices  13.5 us
    all_to_all x1, blocking collectives, on_device(): lax.all_to_all(band_grad[:, inverse, :], 'patch', split_axis=1, concat_ax...  10.7 us
  transfers between devices with their start and end apart: 5, of which 5 were waited for; matrix products, arithmetic and copies ran while one was open for 4% of the time, Pallas kernels for 0%

commit v1 on v0

--- a/solution.py
+++ b/solution.py
@@ -63,6 +63,21 @@
 
 
 def on_device(fields, w_one, bias_one, w_two, neighbour, seam_code, band_order, target, lat_weight):
+
+    def handle_blocks(xin, dev_axis):
+        lanes = jax.lax.axis_size(dev_axis)
+        tray = [xin]
+        w = 0
+        while w < lanes - 1:
+            val2 = jax.lax.ppermute(
+                tray[-1], dev_axis, [(j, (j + 1) % lanes) for j in range(lanes)]
+            )
+            tray.append(val2)
+            w = w + 1
+        z_new = jnp.concatenate(tray[::-1], 0)
+        local_part = jax.lax.axis_index(dev_axis)
+        return jnp.roll(z_new, (local_part + 1) * xin.shape[0], 0)
+
     length = P_SIZE
     span = P_SIZE + 2
     cell_count = P_SIZE * P_SIZE
@@ -160,7 +175,7 @@
             grad_frame[:, 1:-1, -1],
         ]
     )
-    shard_rows = lax.all_gather(frames[None], "patch", axis=0, tiled=True)
+    shard_rows = handle_blocks(frames[None], "patch")
     matched = (neighbour == own_index)[:, :, None] & (
         (seam_code % 4)[:, :, None] == sides[None, None, :]
     )

time: 332 us -> 400 us (1.20)
  waiting for transfers between devices: 110 us -> 182 us
  local copies, waits for them, and re-layouts: 38.7 us -> 46.5 us
  matrix products: 29.4 us -> 22.5 us
  other arithmetic: 12.4 us -> 7.53 us
    ppermute x0 -> x15, waiting for transfers between devices: none -> 99.9 us  [handle_blocks(): jax.lax.ppermute(tray[-1], dev_axis, [(j, (j + 1) % lanes) for j in range...]
    all_gather x1 -> x0, waiting for transfers between devices: 27.6 us -> none  [on_device(): shard_rows = lax.all_gather(frames[None], 'patch', axis=0, tiled=True)]
    concatenate x0 -> x1, local copies, waits for them, and re-layouts: none -> 15.6 us  [handle_blocks(): return jnp.roll(z_new, (local_part + 1) * xin.shape[0], 0)]
    dot_general x9, matrix products: 8.61 us -> 2.67 us  [on_device(): lax.dot_general(grad_wide, h_taps[idx], (((1,), (1,)), ((), ())), preferr...]
    unnamed x47 -> x77, local copies, waits for them, and re-layouts: 10.4 us -> 12.2 us
    unnamed x5 -> x4, waiting for transfers between devices: 13.5 us -> 13.5 us
  transfers between devices with their start and end apart: 5 -> 19, of which waited for: 5 -> 19; matrix products, arithmetic and copies ran while one was open for 4% -> 2% of each run, Pallas kernels for 0% -> 0%
where the time goes in v1:
time: 400 us; the launch traced here: 398 us
  waiting for transfers between devices  182 us (46%)
  blocking collectives  116 us (29%)
  local copies, waits for them, and re-layouts  46.5 us (12%)
  matrix products  22.5 us (6%)
  between operations  16.7 us (4%)
  other arithmetic  7.53 us (2%)
  starting transfers between devices  5.84 us (1%)
    ppermute x15, waiting for transfers between devices, handle_blocks(): jax.lax.ppermute(tray[-1], dev_axis, [(j, (j + 1) % lanes) for j in range...  99.9 us
    psum x1, blocking collectives, on_device(): lax.psum(partial_loss, ('patch', 'chan')) / (patch_count * cell_count * C)  37.3 us
    all_gather x1, waiting for transfers between devices, on_device(): lax.all_gather(edges_of(hidden_grid)[None], 'patch', axis=0, tiled=True)  35 us
    psum x1, blocking collectives, on_device(): lax.psum((one_local, two_local, bias_local), 'patch')  32 us
    psum x1, waiting for transfers between devices, on_device(): lax.psum((one_local, two_local, bias_local), 'patch')  24.9 us
    all_gather x1, blocking collectives, on_device(): lax.all_gather(edges_of(grid)[None], 'patch', axis=0, tiled=True)  23.5 us
    concatenate x1, local copies, waits for them, and re-layouts, handle_blocks(): return jnp.roll(z_new, (local_part + 1) * xin.shape[0], 0)  15.6 us
    unnamed x4, waiting for transfers between devices  13.5 us
  transfers between devices with their start and end apart: 19, of which 19 were waited for; matrix products, arithmetic and copies ran while one was open for 2% of the time, Pallas kernels for 0%

profile of v1, /device:TPU:0, one launch (start us, length us, event | category | flops | bytes accessed | tf_op | source)
XLA Modules:
  0.0 397.6 jit_solution(9625856158023632429)
XLA Ops:
  7.2 7.4 %all-gather = bf16[1,128,1024]{2,1,0:T(8,128)(2,1)S(1)} all-gather(bf16[1,64,1024]{2,1,0:T(8,128)(2,1)} %param.33), channel_id=2, replica_groups=mesh['patch'=16,'chan'=2] {'chan'}, dimensions={1}, use_global_device_ids=true | all-gather | bytes 393216 | tf_op jit(solution)/shard_map/all_gather | solution.py:105
  15.8 23.5 %all-gather.1 = bf16[64,128,32]{1,2,0:T(8,128)(2,1)S(1)} all-gather(bf16[4,128,32]{1,2,0:T(8,128)(2,1)S(1)} %pad_maximum_fusion.2), channel_id=3, replica_groups=mesh['patch'=16,'chan'=2] {'patch'}, dimensions={0}, use_global_device_ids=true | all-gather | bytes 557056 | tf_op jit(solution)/shard_map/all_gather | solution.py:107
  50.1 35.0 %all-gather.5.cloned.1.call-done = bf16[64,256,32]{1,2,0:T(8,128)(2,1)} async-done(((bf16[4,256,32]{1,2,0:T(8,128)(2,1)}), bf16[64,256,32]{1,2,0:T(8,128)(2,1)}) %all-gather.5.cloned.1.call-update) | async-done | bytes 1048592 | tf_op jit(solution)/shard_map/all_gather | solution.py:115
  85.0 2.0 convolution_bitcast_fusion.27
  94.8 13.4 %reduce-scatter.4.cloned.1.call-done = f32[64,1024]{1,0:T(8,128)} async-done(((f32[128,1024]{1,0:T(8,128)}), f32[64,1024]{1,0:T(8,128)}) %reduce-scatter.4.cloned.1.call-update) | async-done | bytes 262160
  110.7 5.6 %all-to-all-start = ((f32[16,1,4096]{2,1,0:T(1,128)}), f32[16,1,4096]{2,1,0:T(1,128)S(1)}, u32[]{:S(2)}, u32[]{:S(2)}) async-start(f32[16,1,4096]{2,1,0:T(1,128)} %reshape.634), calls=%async_computation | async-start | bytes 524288 | tf_op jit(solution)/shard_map/all_to_all | solution.py:130
  117.5 8.9 %all-to-all-done = f32[16,1,4096]{2,1,0:T(1,128)S(1)} async-done(((f32[16,1,4096]{2,1,0:T(1,128)}), f32[16,1,4096]{2,1,0:T(1,128)S(1)}, u32[]{:S(2)}, u32[]{:S(2)}) %all-to-all-start) | async-done | bytes 262176 | tf_op jit(solution)/shard_map/all_to_all | solution.py:130
  130.1 10.7 %all_to_all.10 = bf16[16,2,2048]{2,1,0:T(2,128)(2,1)S(1)} all-to-all(bf16[16,2,2048]{2,1,0:T(2,128)(2,1)S(1)} %reshape.636), channel_id=1, replica_groups=mesh['patch'=16,'chan'=2] {'patch'}, dimensions={0} | all-to-all | bytes 262144 | tf_op jit(solution)/shard_map/all_to_all | solution.py:144
  141.4 5.6 %all_gather.15 = bf16[128,1024]{1,0:T(8,128)(2,1)S(1)} all-gather(bf16[64,1024]{1,0:T(8,128)(2,1)S(1)} %reshape.572), channel_id=1, replica_groups=mesh['patch'=16,'chan'=2] {'chan'}, dimensions={0}, use_global_device_ids=true | all-gather | bytes 393216 | tf_op jit(solution)/shard_map/all_gather | solution.py:149
  154.5 7.1 %collective-permute-done = f32[1,4,256,32]{2,0,1,3:T(1,128)S(1)} collective-permute-done((f32[1,4,256,32]{2,0,1,3:T(1,128)S(1)}, f32[1,4,256,32]{2,0,1,3:T(1,128)S(1)}, u32[]{:S(2)}, u32[]{:S(2)}) %collective-permute-start) | collective-permute-done | bytes 131104 | tf_op jit(solution)/shard_map/ppermute | solution.py:72
  161.5 7.2 %collective-permute-done.1 = f32[1,4,256,32]{2,0,1,3:T(1,128)} collective-permute-done((f32[1,4,256,32]{2,0,1,3:T(1,128)S(1)}, f32[1,4,256,32]{2,0,1,3:T(1,128)}, u32[]{:S(2)}, u32[]{:S(2)}) %collective-permute-start.1) | collective-permute-done | bytes 131104 | tf_op jit(solution)/shard_map/ppermute | solution.py:72
  168.7 7.3 %collective-permute-done.2 = f32[1,4,256,32]{2,0,1,3:T(1,128)S(1)} collective-permute-done((f32[1,4,256,32]{2,0,1,3:T(1,128)}, f32[1,4,256,32]{2,0,1,3:T(1,128)S(1)}, u32[]{:S(2)}, u32[]{:S(2)}) %collective-permute-start.2) | collective-permute-done | bytes 131104 | tf_op jit(solution)/shard_map/ppermute | solution.py:72
  176.0 7.1 %collective-permute-done.3 = f32[1,4,256,32]{2,0,1,3:T(1,128)S(1)} collective-permute-done((f32[1,4,256,32]{2,0,1,3:T(1,128)S(1)}, f32[1,4,256,32]{2,0,1,3:T(1,128)S(1)}, u32[]{:S(2)}, u32[]{:S(2)}) %collective-permute-start.3) | collective-permute-done | bytes 131104 | tf_op jit(solution)/shard_map/ppermute | solution.py:72
  183.7 6.5 %collective-permute-done.4 = f32[1,4,256,32]{2,0,1,3:T(1,128)S(1)} collective-permute-done((f32[1,4,256,32]{2,0,1,3:T(1,128)S(1)}, f32[1,4,256,32]{2,0,1,3:T(1,128)S(1)}, u32[]{:S(2)}, u32[]{:S(2)}) %collective-permute-start.4) | collective-permute-done | bytes 131104 | tf_op jit(solution)/shard_map/ppermute | solution.py:72
  190.3 1.5 slice.614
  192.4 4.9 %collective-permute-done.5 = f32[1,4,256,32]{2,0,1,3:T(1,128)S(1)} collective-permute-done((f32[1,4,256,32]{2,0,1,3:T(1,128)S(1)}, f32[1,4,256,32]{2,0,1,3:T(1,128)S(1)}, u32[]{:S(2)}, u32[]{:S(2)}) %collective-permute-start.5) | collective-permute-done | bytes 131104 | tf_op jit(solution)/shard_map/ppermute | solution.py:72
  197.6 6.8 %collective-permute-done.6 = f32[1,4,256,32]{2,0,1,3:T(1,128)S(1)} collective-permute-done((f32[1,4,256,32]{2,0,1,3:T(1,128)S(1)}, f32[1,4,256,32]{2,0,1,3:T(1,128)S(1)}, u32[]{:S(2)}, u32[]{:S(2)}) %collective-permute-start.6) | collective-permute-done | bytes 131104 | tf_op jit(solution)/shard_map/ppermute | solution.py:72
  204.7 6.8 %collective-permute-done.7 = f32[1,4,256,32]{2,0,1,3:T(1,128)S(1)} collective-permute-done((f32[1,4,256,32]{2,0,1,3:T(1,128)S(1)}, f32[1,4,256,32]{2,0,1,3:T(1,128)S(1)}, u32[]{:S(2)}, u32[]{:S(2)}) %collective-permute-start.7) | collective-permute-done | bytes 131104 | tf_op jit(solution)/shard_map/ppermute | solution.py:72
  211.8 6.8 %collective-permute-done.8 = f32[1,4,256,32]{2,0,1,3:T(1,128)S(1)} collective-permute-done((f32[1,4,256,32]{2,0,1,3:T(1,128)S(1)}, f32[1,4,256,32]{2,0,1,3:T(1,128)S(1)}, u32[]{:S(2)}, u32[]{:S(2)}) %collective-permute-start.8) | collective-permute-done | bytes 131104 | tf_op jit(solution)/shard_map/ppermute | solution.py:72
  218.9 6.8 %collective-permute-done.9 = f32[1,4,256,32]{2,0,1,3:T(1,128)S(1)} collective-permute-done((f32[1,4,256,32]{2,0,1,3:T(1,128)S(1)}, f32[1,4,256,32]{2,0,1,3:T(1,128)S(1)}, u32[]{:S(2)}, u32[]{:S(2)}) %collective-permute-start.9) | collective-permute-done | bytes 131104 | tf_op jit(solution)/shard_map/ppermute | solution.py:72
  226.0 6.8 %collective-permute-done.10 = f32[1,4,256,32]{2,0,1,3:T(1,128)S(1)} collective-permute-done((f32[1,4,256,32]{2,0,1,3:T(1,128)S(1)}, f32[1,4,256,32]{2,0,1,3:T(1,128)S(1)}, u32[]{:S(2)}, u32[]{:S(2)}) %collective-permute-start.10) | collective-permute-done | bytes 131104 | tf_op jit(solution)/shard_map/ppermute | solution.py:72
  233.1 6.8 %collective-permute-done.11 = f32[1,4,256,32]{2,0,1,3:T(1,128)S(1)} collective-permute-done((f32[1,4,256,32]{2,0,1,3:T(1,128)S(1)}, f32[1,4,256,32]{2,0,1,3:T(1,128)S(1)}, u32[]{:S(2)}, u32[]{:S(2)}) %collective-permute-start.11) | collective-permute-done | bytes 131104 | tf_op jit(solution)/shard_map/ppermute | solution.py:72
  240.2 6.8 %collective-permute-done.12 = f32[1,4,256,32]{2,0,1,3:T(1,128)S(1)} collective-permute-done((f32[1,4,256,32]{2,0,1,3:T(1,128)S(1)}, f32[1,4,256,32]{2,0,1,3:T(1,128)S(1)}, u32[]{:S(2)}, u32[]{:S(2)}) %collective-permute-start.12) | collective-permute-done | bytes 131104 | tf_op jit(solution)/shard_map/ppermute | solution.py:72
  247.3 6.8 %collective-permute-done.13 = f32[1,4,256,32]{2,0,1,3:T(1,128)S(1)} collective-permute-done((f32[1,4,256,32]{2,0,1,3:T(1,128)S(1)}, f32[1,4,256,32]{2,0,1,3:T(1,128)S(1)}, u32[]{:S(2)}, u32[]{:S(2)}) %collective-permute-start.13) | collective-permute-done | bytes 131104 | tf_op jit(solution)/shard_map/ppermute | solution.py:72
  255.7 5.5 %collective-permute-done.14 = f32[1,4,256,32]{2,0,1,3:T(1,128)} collective-permute-done((f32[1,4,256,32]{2,0,1,3:T(1,128)S(1)}, f32[1,4,256,32]{2,0,1,3:T(1,128)}, u32[]{:S(2)}, u32[]{:S(2)}) %collective-permute-start.14) | collective-permute-done | bytes 131104 | tf_op jit(solution)/shard_map/ppermute | solution.py:72
  261.3 15.6 %concatenate.34 = f32[32,4,256,32]{2,0,1,3:T(8,128)} concatenate(f32[1,4,256,32]{2,0,1,3:T(1,128)} %collective-permute-done.14, f32[1,4,256,32]{2,0,1,3:T(1,128)} %copy-done.19, f32[1,4,256,32]{2,0,1,3:T(1,128)} %copy-done.18, f32[1,4,256,32]{2,0,1,3:T(1,128)} %copy-done.17, f32[1,4,256,32]{2,0,1,3:T(1,128)} %copy-done.16, f32[1,4,256,32]{2,0,1,3:T(1,128)} %copy-done.15, ...), dimensions={0} | concatenate | bytes 8388608 | tf_op jit(solution)/shard_map/jit(_roll_dynamic)/concatenate | solution.py:79
  276.9 2.9 fusion.6
  279.7 2.9 fusion.9
  291.6 37.3 %psum.28 = f32[]{:T(128)} all-reduce(f32[]{:T(128)} %fusion.56), channel_id=1, replica_groups=mesh['patch'=16,'chan'=2] {'patch','chan'}, use_global_device_ids=true, to_apply=%region_2.3 | all-reduce | flops 1 | bytes 8 | tf_op jit(solution)/shard_map/psum | solution.py:148
  329.6 32.0 %psum.31 = f32[256]{0:T(256)} all-reduce(f32[256]{0:T(256)S(1)} %get-tuple-element.150), channel_id=1, replica_groups=mesh['patch'=16,'chan'=2] {'patch'}, use_global_device_ids=true, to_apply=%region_7.8 | all-reduce | flops 256 | bytes 2048 | tf_op jit(solution)/shard_map/psum | solution.py:212
  361.6 24.9 %all-reduce.18.cloned.1.call-done = (f32[9,256,128]{2,1,0:T(8,128)}, f32[9,128,256]{2,1,0:T(8,128)}) async-done(((f32[9,256,128]{2,1,0:T(8,128)}, f32[9,128,256]{2,1,0:T(8,128)}), (f32[9,256,128]{2,1,0:T(8,128)}, f32[9,128,256]{2,1,0:T(8,128)})) %all-reduce.18.cloned.1.call-update) | async-done | bytes 2359312 | tf_op jit(solution)/shard_map/psum | solution.py:212
  386.5 2.5 copy.196
  (227 shorter events, 49.6 us)
Async XLA Ops:
  7.2 77.9 %all-gather.5.cloned.1.call-start = ((), (), s32[]{:S(2)}) async-start(), calls=%async_computation.3 | async-start | bytes 1114112 | tf_op jit(solution)/shard_map/all_gather | solution.py:115
  49.7 58.6 %reduce-scatter.4.cloned.1.call-start = ((), (), s32[]{:S(2)}) async-start(), calls=%async_computation.4 | async-start | bytes 786432
  110.7 15.7 %all-to-all-start = ((f32[16,1,4096]{2,1,0:T(1,128)}), f32[16,1,4096]{2,1,0:T(1,128)S(1)}, u32[]{:S(2)}, u32[]{:S(2)}) async-start(f32[16,1,4096]{2,1,0:T(1,128)} %reshape.634), calls=%async_computation | async-start | bytes 524288 | tf_op jit(solution)/shard_map/all_to_all | solution.py:130
  116.3 270.1 %all-reduce.18.cloned.1.call-start = ((), (), s32[]{:S(2)}) async-start(), calls=%async_computation.5 | async-start | bytes 4718592 | tf_op jit(solution)/shard_map/psum | solution.py:212
  150.9 32.2 %copy-start.23 = (s32[16,4]{0,1:T(4,128)S(1)}, s32[16,4]{0,1:T(4,128)}, u32[]{:S(2)}) copy-start(s32[16,4]{0,1:T(4,128)} %param.38) | copy-start | bytes 772
  150.9 32.2 %copy-start.25 = (s32[16,4]{0,1:T(4,128)S(1)}, s32[16,4]{0,1:T(4,128)}, u32[]{:S(2)}) copy-start(s32[16,4]{0,1:T(4,128)} %param.37) | copy-start | bytes 772
  154.4 7.1 %collective-permute-start = (f32[1,4,256,32]{2,0,1,3:T(1,128)S(1)}, f32[1,4,256,32]{2,0,1,3:T(1,128)S(1)}, u32[]{:S(2)}, u32[]{:S(2)}) collective-permute-start(f32[1,4,256,32]{2,0,1,3:T(1,128)S(1)} %broadcast_in_dim.32), channel_id=1, source_target_pairs={{0,2},{2,4},{4,6},{6,8},{8,10},{10,12},{12,14},{14,16},{16,18},{18... | collective-permute-start | bytes 393224 | tf_op jit(solution)/shard_map/ppermute | solution.py:72
  161.5 7.2 %collective-permute-start.1 = (f32[1,4,256,32]{2,0,1,3:T(1,128)S(1)}, f32[1,4,256,32]{2,0,1,3:T(1,128)}, u32[]{:S(2)}, u32[]{:S(2)}) collective-permute-start(f32[1,4,256,32]{2,0,1,3:T(1,128)S(1)} %collective-permute-done), channel_id=1, source_target_pairs={{0,2},{2,4},{4,6},{6,8},{8,10},{10,12},{12,14},{14,16},{16,18},{18... | collective-permute-start | bytes 393224 | tf_op jit(solution)/shard_map/ppermute | solution.py:72
  168.7 7.3 %collective-permute-start.2 = (f32[1,4,256,32]{2,0,1,3:T(1,128)}, f32[1,4,256,32]{2,0,1,3:T(1,128)S(1)}, u32[]{:S(2)}, u32[]{:S(2)}) collective-permute-start(f32[1,4,256,32]{2,0,1,3:T(1,128)} %collective-permute-done.1), channel_id=1, source_target_pairs={{0,2},{2,4},{4,6},{6,8},{8,10},{10,12},{12,14},{14,16},{16,18},{18... | collective-permute-start | bytes 393224 | tf_op jit(solution)/shard_map/ppermute | solution.py:72
  176.0 14.2 %copy-start.8 = (f32[1,4,256,32]{2,0,1,3:T(1,128)}, f32[1,4,256,32]{2,0,1,3:T(1,128)S(1)}, u32[]{:S(2)}) copy-start(f32[1,4,256,32]{2,0,1,3:T(1,128)S(1)} %collective-permute-done.2) | copy-start | bytes 393220
  176.0 7.1 %collective-permute-start.3 = (f32[1,4,256,32]{2,0,1,3:T(1,128)S(1)}, f32[1,4,256,32]{2,0,1,3:T(1,128)S(1)}, u32[]{:S(2)}, u32[]{:S(2)}) collective-permute-start(f32[1,4,256,32]{2,0,1,3:T(1,128)S(1)} %collective-permute-done.2), channel_id=1, source_target_pairs={{0,2},{2,4},{4,6},{6,8},{8,10},{10,12},{12,14},{14,16},{16,18},{18... | collective-permute-start | bytes 393224 | tf_op jit(solution)/shard_map/ppermute | solution.py:72
  183.1 7.1 %copy-start.9 = (f32[1,4,256,32]{2,0,1,3:T(1,128)}, f32[1,4,256,32]{2,0,1,3:T(1,128)S(1)}, u32[]{:S(2)}) copy-start(f32[1,4,256,32]{2,0,1,3:T(1,128)S(1)} %collective-permute-done.3) | copy-start | bytes 393220
  183.1 7.1 %collective-permute-start.4 = (f32[1,4,256,32]{2,0,1,3:T(1,128)S(1)}, f32[1,4,256,32]{2,0,1,3:T(1,128)S(1)}, u32[]{:S(2)}, u32[]{:S(2)}) collective-permute-start(f32[1,4,256,32]{2,0,1,3:T(1,128)S(1)} %collective-permute-done.3), channel_id=1, source_target_pairs={{0,2},{2,4},{4,6},{6,8},{8,10},{10,12},{12,14},{14,16},{16,18},{18... | collective-permute-start | bytes 393224 | tf_op jit(solution)/shard_map/ppermute | solution.py:72
  190.2 7.1 %collective-permute-start.5 = (f32[1,4,256,32]{2,0,1,3:T(1,128)S(1)}, f32[1,4,256,32]{2,0,1,3:T(1,128)S(1)}, u32[]{:S(2)}, u32[]{:S(2)}) collective-permute-start(f32[1,4,256,32]{2,0,1,3:T(1,128)S(1)} %collective-permute-done.4), channel_id=1, source_target_pairs={{0,2},{2,4},{4,6},{6,8},{8,10},{10,12},{12,14},{14,16},{16,18},{18... | collective-permute-start | bytes 393224 | tf_op jit(solution)/shard_map/ppermute | solution.py:72
  197.3 14.5 %copy-start.11 = (f32[1,4,256,32]{2,0,1,3:T(1,128)}, f32[1,4,256,32]{2,0,1,3:T(1,128)S(1)}, u32[]{:S(2)}) copy-start(f32[1,4,256,32]{2,0,1,3:T(1,128)S(1)} %collective-permute-done.5) | copy-start | bytes 393220
  197.3 7.1 %collective-permute-start.6 = (f32[1,4,256,32]{2,0,1,3:T(1,128)S(1)}, f32[1,4,256,32]{2,0,1,3:T(1,128)S(1)}, u32[]{:S(2)}, u32[]{:S(2)}) collective-permute-start(f32[1,4,256,32]{2,0,1,3:T(1,128)S(1)} %collective-permute-done.5), channel_id=1, source_target_pairs={{0,2},{2,4},{4,6},{6,8},{8,10},{10,12},{12,14},{14,16},{16,18},{18... | collective-permute-start | bytes 393224 | tf_op jit(solution)/shard_map/ppermute | solution.py:72
  204.4 7.4 %copy-start.12 = (f32[1,4,256,32]{2,0,1,3:T(1,128)}, f32[1,4,256,32]{2,0,1,3:T(1,128)S(1)}, u32[]{:S(2)}) copy-start(f32[1,4,256,32]{2,0,1,3:T(1,128)S(1)} %collective-permute-done.6) | copy-start | bytes 393220
  204.4 7.1 %collective-permute-start.7 = (f32[1,4,256,32]{2,0,1,3:T(1,128)S(1)}, f32[1,4,256,32]{2,0,1,3:T(1,128)S(1)}, u32[]{:S(2)}, u32[]{:S(2)}) collective-permute-start(f32[1,4,256,32]{2,0,1,3:T(1,128)S(1)} %collective-permute-done.6), channel_id=1, source_target_pairs={{0,2},{2,4},{4,6},{6,8},{8,10},{10,12},{12,14},{14,16},{16,18},{18... | collective-permute-start | bytes 393224 | tf_op jit(solution)/shard_map/ppermute | solution.py:72
  211.5 7.4 %copy-start.13 = (f32[1,4,256,32]{2,0,1,3:T(1,128)}, f32[1,4,256,32]{2,0,1,3:T(1,128)S(1)}, u32[]{:S(2)}) copy-start(f32[1,4,256,32]{2,0,1,3:T(1,128)S(1)} %collective-permute-done.7) | copy-start | bytes 393220
  211.5 7.1 %collective-permute-start.8 = (f32[1,4,256,32]{2,0,1,3:T(1,128)S(1)}, f32[1,4,256,32]{2,0,1,3:T(1,128)S(1)}, u32[]{:S(2)}, u32[]{:S(2)}) collective-permute-start(f32[1,4,256,32]{2,0,1,3:T(1,128)S(1)} %collective-permute-done.7), channel_id=1, source_target_pairs={{0,2},{2,4},{4,6},{6,8},{8,10},{10,12},{12,14},{14,16},{16,18},{18... | collective-permute-start | bytes 393224 | tf_op jit(solution)/shard_map/ppermute | solution.py:72
  218.6 7.4 %copy-start.14 = (f32[1,4,256,32]{2,0,1,3:T(1,128)}, f32[1,4,256,32]{2,0,1,3:T(1,128)S(1)}, u32[]{:S(2)}) copy-start(f32[1,4,256,32]{2,0,1,3:T(1,128)S(1)} %collective-permute-done.8) | copy-start | bytes 393220
  218.6 7.1 %collective-permute-start.9 = (f32[1,4,256,32]{2,0,1,3:T(1,128)S(1)}, f32[1,4,256,32]{2,0,1,3:T(1,128)S(1)}, u32[]{:S(2)}, u32[]{:S(2)}) collective-permute-start(f32[1,4,256,32]{2,0,1,3:T(1,128)S(1)} %collective-permute-done.8), channel_id=1, source_target_pairs={{0,2},{2,4},{4,6},{6,8},{8,10},{10,12},{12,14},{14,16},{16,18},{18... | collective-permute-start | bytes 393224 | tf_op jit(solution)/shard_map/ppermute | solution.py:72
  225.7 7.4 %copy-start.15 = (f32[1,4,256,32]{2,0,1,3:T(1,128)}, f32[1,4,256,32]{2,0,1,3:T(1,128)S(1)}, u32[]{:S(2)}) copy-start(f32[1,4,256,32]{2,0,1,3:T(1,128)S(1)} %collective-permute-done.9) | copy-start | bytes 393220
  225.7 7.1 %collective-permute-start.10 = (f32[1,4,256,32]{2,0,1,3:T(1,128)S(1)}, f32[1,4,256,32]{2,0,1,3:T(1,128)S(1)}, u32[]{:S(2)}, u32[]{:S(2)}) collective-permute-start(f32[1,4,256,32]{2,0,1,3:T(1,128)S(1)} %collective-permute-done.9), channel_id=1, source_target_pairs={{0,2},{2,4},{4,6},{6,8},{8,10},{10,12},{12,14},{14,16},{16,18},{18... | collective-permute-start | bytes 393224 | tf_op jit(solution)/shard_map/ppermute | solution.py:72
  232.8 7.4 %copy-start.16 = (f32[1,4,256,32]{2,0,1,3:T(1,128)}, f32[1,4,256,32]{2,0,1,3:T(1,128)S(1)}, u32[]{:S(2)}) copy-start(f32[1,4,256,32]{2,0,1,3:T(1,128)S(1)} %collective-permute-done.10) | copy-start | bytes 393220
  232.8 7.1 %collective-permute-start.11 = (f32[1,4,256,32]{2,0,1,3:T(1,128)S(1)}, f32[1,4,256,32]{2,0,1,3:T(1,128)S(1)}, u32[]{:S(2)}, u32[]{:S(2)}) collective-permute-start(f32[1,4,256,32]{2,0,1,3:T(1,128)S(1)} %collective-permute-done.10), channel_id=1, source_target_pairs={{0,2},{2,4},{4,6},{6,8},{8,10},{10,12},{12,14},{14,16},{16,18},{18... | collective-permute-start | bytes 393224 | tf_op jit(solution)/shard_map/ppermute | solution.py:72
  239.9 7.4 %copy-start.17 = (f32[1,4,256,32]{2,0,1,3:T(1,128)}, f32[1,4,256,32]{2,0,1,3:T(1,128)S(1)}, u32[]{:S(2)}) copy-start(f32[1,4,256,32]{2,0,1,3:T(1,128)S(1)} %collective-permute-done.11) | copy-start | bytes 393220
  239.9 7.1 %collective-permute-start.12 = (f32[1,4,256,32]{2,0,1,3:T(1,128)S(1)}, f32[1,4,256,32]{2,0,1,3:T(1,128)S(1)}, u32[]{:S(2)}, u32[]{:S(2)}) collective-permute-start(f32[1,4,256,32]{2,0,1,3:T(1,128)S(1)} %collective-permute-done.11), channel_id=1, source_target_pairs={{0,2},{2,4},{4,6},{6,8},{8,10},{10,12},{12,14},{14,16},{16,18},{18... | collective-permute-start | bytes 393224 | tf_op jit(solution)/shard_map/ppermute | solution.py:72
  247.0 7.4 %copy-start.18 = (f32[1,4,256,32]{2,0,1,3:T(1,128)}, f32[1,4,256,32]{2,0,1,3:T(1,128)S(1)}, u32[]{:S(2)}) copy-start(f32[1,4,256,32]{2,0,1,3:T(1,128)S(1)} %collective-permute-done.12) | copy-start | bytes 393220
  247.0 7.1 %collective-permute-start.13 = (f32[1,4,256,32]{2,0,1,3:T(1,128)S(1)}, f32[1,4,256,32]{2,0,1,3:T(1,128)S(1)}, u32[]{:S(2)}, u32[]{:S(2)}) collective-permute-start(f32[1,4,256,32]{2,0,1,3:T(1,128)S(1)} %collective-permute-done.12), channel_id=1, source_target_pairs={{0,2},{2,4},{4,6},{6,8},{8,10},{10,12},{12,14},{14,16},{16,18},{18... | collective-permute-start | bytes 393224 | tf_op jit(solution)/shard_map/ppermute | solution.py:72
  254.1 7.2 %collective-permute-start.14 = (f32[1,4,256,32]{2,0,1,3:T(1,128)S(1)}, f32[1,4,256,32]{2,0,1,3:T(1,128)}, u32[]{:S(2)}, u32[]{:S(2)}) collective-permute-start(f32[1,4,256,32]{2,0,1,3:T(1,128)S(1)} %collective-permute-done.13), channel_id=1, source_target_pairs={{0,2},{2,4},{4,6},{6,8},{8,10},{10,12},{12,14},{14,16},{16,18},{18... | collective-permute-start | bytes 393224 | tf_op jit(solution)/shard_map/ppermute | solution.py:72
  255.7 21.2 %copy-start.27 = (pred[16,4]{0,1:T(4,128)(4,1)S(1)}, pred[16,4]{0,1:T(4,128)(4,1)}, u32[]{:S(2)}) copy-start(pred[16,4]{0,1:T(4,128)(4,1)} %get-tuple-element.172) | copy-start | bytes 196
  (16 other events, 38.7 us)
Sparse Core Ops, SparseCore 0:
  49.8 35.2 all-gather.4
  94.7 13.4 reduce-scatter.3
  290.1 96.2 all-reduce.17
